TPU v7x, 32 devices: a whole 2x2x4 slice. The times are simulated.
32 devices in a mesh: inst: 8 (over z, y), space: 4 (over x, core).
Axes of the slice: x: 2, y: 2, z: 4, core: 2. Of those that a mesh axis runs over, the one named last changes fastest.
Arguments:
- state: float32 [32, 320, 512], P('inst', None, 'space'), may hold values from -6 to 6
- forcing: float32 [32, 320, 512], P('inst', None, 'space'), may hold values from -6 to 6
- flux_jac: float32 [3, 5, 5], replicated, may hold values from -0.875 to 0.875
- jacobi_inv: float32 [32, 320, 320], P('inst'), may hold values from -0.01 to 0.03
- cross_nbr: int32 [4, 64], replicated, may hold values from 0 to 63, as said below
- lower_match: int32 [32, 4, 64], P('inst', 'space'), may hold values from 0 to 63, as said below
Outputs:
- residual: float32 [32, 320, 512], P('inst', None, 'space')
- updated: float32 [32, 320, 512], P('inst', None, 'space')
Inputs may be any that keep to these rules, and one draw needn't show every extreme that they name: `cross_nbr`: the cells form a grid of 8 by 8, periodic in both directions, in an order drawn from the seed; if row 0 names n for cell c then row 1 names c for n, and likewise rows 2 and 3. lower_match[t, p] is the identity except at the sliding interface p = 4 // 2, where it is the cyclic pitch shift of the cross_nbr grid by (t * 8 // 32 + r) % 8 rows, with one offset r drawn from the seed: the cell below that faces c is the one reached from c by that many steps through row 1 of cross_nbr.
All inputs are finite; a program needn't handle non-finite values.
Results may differ from a plain program's by a relative error of at most 0.0003.
Values sent between devices are 32-bit elements; how exact they have to be, the bound alone decides.
A program may use at most 128 MiB of HBM per device.

v0:
```python
import math

import jax
import jax.numpy as jnp
import numpy as np
from jax import lax
from jax.sharding import PartitionSpec as P

VARS = 5
NODE1 = 4
PITCH_ELEMENTS = 8
EZ = 8
SWEEPS = 2


dissipation = 0.6
frequency = 0.25


def with_halo(block, sides, width):
    for axis, dim in sides:
        count = lax.axis_size(axis)
        forward = [(i, i + 1) for i in range(count - 1)]
        backward = [(target, source) for source, target in forward]
        low = lax.ppermute(
            lax.slice_in_dim(block, block.shape[dim] - width, None, axis=dim), axis, forward
        )
        high = lax.ppermute(lax.slice_in_dim(block, 0, width, axis=dim), axis, backward)
        block = jnp.concatenate([low, block, high], axis=dim)
    return block


def lobatto_derivative(count_of_nodes):
    inner_point = math.sqrt(0.2)
    points = np.array([-1.0, -inner_point, inner_point, 1.0])
    barycentric = np.ones(count_of_nodes)
    for first_index in range(count_of_nodes):
        for second_index in range(count_of_nodes):
            if first_index != second_index:
                barycentric[first_index] = barycentric[first_index] / (
                    points[first_index] - points[second_index]
                )
    table = np.zeros((count_of_nodes, count_of_nodes))
    for first_index in range(count_of_nodes):
        for second_index in range(count_of_nodes):
            if first_index != second_index:
                table[first_index, second_index] = (
                    barycentric[second_index]
                    / barycentric[first_index]
                    / (points[first_index] - points[second_index])
                )
        table[first_index, first_index] = -np.sum(table[first_index])
    return table


def time_matrix(count):
    pitch_offset = (
        jnp.arange(count, dtype=jnp.int32)[:, None] - jnp.arange(count, dtype=jnp.int32)[None, :]
    )
    parity = 1.0 - 2.0 * (pitch_offset % 2).astype(jnp.float32)
    angle = jnp.pi * pitch_offset.astype(jnp.float32) / count
    safe_tan = jnp.where(pitch_offset == 0, 1.0, jnp.tan(angle))
    return jnp.where(pitch_offset == 0, 0.0, 0.5 * frequency * parity / safe_tan)


def differentiate(stack):
    matrix = time_matrix(stack.shape[0])
    return jnp.einsum("ts,sbe->tbe", matrix, stack, precision=lax.Precision.HIGHEST)


def time_rates(field):
    return lax.all_to_all(
        differentiate(lax.all_to_all(field, "inst", split_axis=2, concat_axis=0, tiled=True)),
        "inst",
        split_axis=0,
        concat_axis=2,
        tiled=True,
    )


def permute_cells(values, index):
    return jnp.take_along_axis(values, index[:, None, :], axis=2)


def face_term(plus, minus, jacobian, sign):
    matrix = sign * jacobian - dissipation * jnp.eye(jacobian.shape[0], dtype=jnp.float32)
    return jnp.einsum("wv,tvabe->twabe", matrix, plus - minus, precision=lax.Precision.HIGHEST)


def space_residual(field, flux_jac, derivative, neighbours, matching_cells, inverse_cells):
    local_times, block, elements = field.shape
    nodes = NODE1
    width = VARS
    cells = PITCH_ELEMENTS * EZ
    face_size = width * nodes * nodes
    highest = lax.Precision.HIGHEST
    reshaped_array = field.reshape(local_times, width, nodes, nodes, nodes, elements)
    low_x = reshaped_array[:, :, 0]
    high_x = reshaped_array[:, :, nodes - 1]
    first_trace = low_x[..., :cells].reshape(local_times, face_size, cells)
    last_trace = high_x[..., elements - cells :].reshape(local_times, face_size, cells)
    outgoing = jnp.concatenate([permute_cells(first_trace, inverse_cells), last_trace], axis=2)
    received = with_halo(outgoing, (("space", 2),), cells)
    from_below = received[:, :, :cells]
    from_above = received[:, :, 3 * cells :]
    from_below = permute_cells(from_below, matching_cells).reshape(
        local_times, width, nodes, nodes, cells
    )
    from_above = from_above.reshape(local_times, width, nodes, nodes, cells)
    plus_low_x = jnp.concatenate([from_below, high_x[..., : elements - cells]], axis=4)
    plus_high_x = jnp.concatenate([low_x[..., cells:], from_above], axis=4)
    along_x = jnp.einsum("ai,tvijke->tvajke", derivative, reshaped_array, precision=highest)
    along_y = jnp.einsum("aj,tvijke->tviake", derivative, reshaped_array, precision=highest)
    along_z = jnp.einsum("ak,tvijke->tvijae", derivative, reshaped_array, precision=highest)
    volume = jnp.einsum("wv,tvijke->twijke", flux_jac[0], along_x, precision=highest)
    volume = volume + jnp.einsum("wv,tvijke->twijke", flux_jac[1], along_y, precision=highest)
    volume = volume + jnp.einsum("wv,tvijke->twijke", flux_jac[2], along_z, precision=highest)
    scale = nodes * (nodes - 1) / 4.0
    low_y = reshaped_array[:, :, :, 0]
    high_y = reshaped_array[:, :, :, nodes - 1]
    low_z = reshaped_array[:, :, :, :, 0]
    high_z = reshaped_array[:, :, :, :, nodes - 1]
    volume = volume.at[:, :, 0].add(scale * face_term(plus_low_x, low_x, flux_jac[0], -1.0))
    volume = volume.at[:, :, nodes - 1].add(
        scale * face_term(plus_high_x, high_x, flux_jac[0], 1.0)
    )
    volume = volume.at[:, :, :, 0].add(
        scale * face_term(jnp.take(high_y, neighbours[0], axis=4), low_y, flux_jac[1], -1.0)
    )
    volume = volume.at[:, :, :, nodes - 1].add(
        scale * face_term(jnp.take(low_y, neighbours[1], axis=4), high_y, flux_jac[1], 1.0)
    )
    volume = volume.at[:, :, :, :, 0].add(
        scale * face_term(jnp.take(high_z, neighbours[2], axis=4), low_z, flux_jac[2], -1.0)
    )
    volume = volume.at[:, :, :, :, nodes - 1].add(
        scale * face_term(jnp.take(low_z, neighbours[3], axis=4), high_z, flux_jac[2], 1.0)
    )
    return volume.reshape(local_times, block, elements)


def body(state, forcing, flux_jac, jacobi_inv, cross_nbr, lower_match):
    local_times, block, elements = state.shape
    cells = PITCH_ELEMENTS * EZ
    derivative = jnp.asarray(lobatto_derivative(NODE1), jnp.float32)
    layer_start = jnp.arange(elements // cells, dtype=jnp.int32) * cells
    neighbours = (layer_start[None, :, None] + cross_nbr[:, None, :]).reshape(4, elements)
    matching_cells = lower_match[:, 0, :]
    inverse_cells = jnp.argsort(matching_cells, axis=-1)
    current = state
    first_residual = state
    for sweep in range(SWEEPS):
        rates = time_rates(current)
        spatial = space_residual(
            current, flux_jac, derivative, neighbours, matching_cells, inverse_cells
        )
        residual = spatial + rates - forcing
        if sweep == 0:
            first_residual = residual
        current = current - jnp.einsum(
            "tpq,tqe->tpe", jacobi_inv, residual, precision=lax.Precision.HIGHEST
        )
    return (first_residual, current)


def solution(mesh):
    return jax.shard_map(
        body,
        mesh=mesh,
        in_specs=(
            P("inst", None, "space"),
            P("inst", None, "space"),
            P(),
            P("inst", None, None),
            P(),
            P("inst", "space", None),
        ),
        out_specs=(P("inst", None, "space"), P("inst", None, "space")),
        check_vma=False,
    )
```

profile of v0, /device:TPU:0, one launch (start us, length us, event | category | flops | bytes accessed | tf_op | source)
XLA Modules:
  0.0 343.8 jit_solution(9277258930535717636)
XLA Ops:
  10.2 3.0 collective-permute-start
  14.4 7.7 %all-to-all-start = ((f32[4,320,128]{1,0,2:T(4,128)}), f32[4,320,128]{1,0,2:T(4,128)}, u32[]{:S(2)}, u32[]{:S(2)}) async-start(f32[4,320,128]{1,0,2:T(4,128)} %copy.355), calls=%async_computation | async-start | bytes 1572864 | tf_op jit(solution)/shard_map/all_to_all | solution.py:73
  29.8 4.5 %copy.455 = f32[4,5,4,4,1,128]{1,3,2,0,5,4:T(4,128)} copy(f32[4,5,4,4,1,128]{5,4,3,2,1,0:T(1,128)} %get-tuple-element.160) | data formatting | bytes 327680
  34.3 4.3 %copy.463 = f32[4,5,4,4,1,128]{1,3,5,2,0,4:T(4,128)} copy(f32[4,5,4,4,1,128]{5,4,3,2,1,0:T(1,128)} %get-tuple-element.160) | data formatting | bytes 327680 | tf_op jit(solution)/shard_map/squeeze | solution.py:121
  38.7 2.4 fusion.145
  41.1 2.4 convolution_add_fusion.3
  45.9 4.6 %copy.451 = f32[4,5,4,1,4,128]{1,4,2,0,5,3:T(4,128)} copy(f32[4,5,4,1,4,128]{5,4,3,2,1,0:T(4,128)} %get-tuple-element.162) | data formatting | bytes 327680
  50.5 4.3 %copy.450 = f32[4,5,4,1,4,128]{1,4,5,2,0,3:T(4,128)} copy(f32[4,5,4,1,4,128]{5,4,3,2,1,0:T(4,128)} %get-tuple-element.163) | data formatting | bytes 327680
  54.9 3.2 copy.342
  58.1 3.6 %copy.454 = f32[4,5,4,4,1,128]{1,3,5,2,0,4:T(4,128)} copy(f32[4,5,4,4,1,128]{5,4,3,2,1,0:T(1,128)S(1)} %copy-done.19) | data formatting | bytes 327680
  61.7 7.7 %gather_fusion.2 = f32[128,4,5,4,4]{2,4,3,1,0:T(4,128)} fusion(f32[4,5,4,4,128]{1,3,4,2,0:T(4,128)} %bitcast.450, s32[1024]{0:T(1024)S(1)} %pad_clamp_fusion.3), kind=kCustom, calls=%fused_computation.1.clone | custom fusion | bytes 328192 | tf_op jit(solution)/shard_map/jit(_take)/gather | solution.py:128
  69.4 7.7 %gather_fusion.3 = f32[128,4,5,4,4]{2,4,3,1,0:T(4,128)} fusion(f32[4,5,4,4,128]{1,3,4,2,0:T(4,128)} %copy.342, s32[1024]{0:T(1024)S(1)} %pad_clamp_fusion.2), kind=kCustom, calls=%fused_computation.5.clone | custom fusion | bytes 328192 | tf_op jit(solution)/shard_map/jit(_take)/gather | solution.py:131
  77.1 5.9 %bitcast_subtract_fusion.6 = f32[4,5,4,4,128]{1,3,4,2,0:T(4,128)} fusion(f32[128,4,5,4,4]{2,4,3,1,0:T(4,128)} %gather_fusion.3, pred[128]{0:T(512)(128)(4,1)S(1)} %get-tuple-element.189, f32[4,5,4,1,4,128]{1,4,5,2,0,3:T(4,128)} %copy.450), kind=kLoop, calls=%fused_computation.22 | loop fusion | flops 81920 | bytes 491648 | tf_op jit(solution)/shard_map/sub | solution.py:87
  83.1 7.8 %gather_fusion.4 = f32[128,4,5,4,4]{2,4,3,1,0:T(4,128)} fusion(f32[4,5,4,4,128]{1,3,4,2,0:T(4,128)} %bitcast.451, s32[1024]{0:T(1024)S(1)} %pad_clamp_fusion.1), kind=kCustom, calls=%fused_computation.6.clone | custom fusion | bytes 328192 | tf_op jit(solution)/shard_map/jit(_take)/gather | solution.py:134
  90.8 7.7 %gather_fusion.5 = f32[128,4,5,4,4]{2,4,3,1,0:T(4,128)} fusion(f32[4,5,4,4,128]{1,3,4,2,0:T(4,128)} %bitcast.455, s32[1024]{0:T(1024)S(1)} %pad_clamp_fusion), kind=kCustom, calls=%fused_computation.7.clone | custom fusion | bytes 328192 | tf_op jit(solution)/shard_map/jit(_take)/gather | solution.py:137
  98.6 5.9 %bitcast_subtract_fusion.4 = f32[4,5,4,4,128]{1,3,4,2,0:T(4,128)} fusion(f32[128,4,5,4,4]{2,4,3,1,0:T(4,128)} %gather_fusion.5, pred[128]{0:T(512)(128)(4,1)S(1)} %get-tuple-element.187, f32[4,5,4,4,1,128]{1,3,5,2,0,4:T(4,128)} %copy.454), kind=kLoop, calls=%fused_computation.20 | loop fusion | flops 81920 | bytes 491648 | tf_op jit(solution)/shard_map/sub | solution.py:87
  106.0 3.1 bitcast_subtract_fusion.7
  111.0 3.3 bitcast_subtract_fusion.5
  123.8 6.9 %fusion.126 = f32[4,5,4,4,4,128]{5,1,4,3,2,0:T(8,128)} fusion(f32[4,5,4,4,4,128]{5,1,4,3,2,0:T(8,128)} %fusion.134, f32[4,5,4,1,4,128]{5,1,4,2,0,3:T(8,128)S(1)} %slice_bitcast_fusion.2, f32[4,5,4,4,128]{1,3,2,0,4:T(4,128)S(1)} %copy-done.8, f32[1,5,5]{2,0,1:T(1,128)S(1)} %get-tuple-element.177), kind=kOutput, calls=%fused_computation.98 | convolution fusion | flops 2539620 | bytes 589924 | tf_op jit(solution)/shard_map/wv,tvabe->twabe/dot_general | solution.py:87
  138.6 6.4 %all-to-all-start.1 = ((f32[32,320,16]{1,2,0:T(8,128)}), f32[32,320,16]{1,2,0:T(8,128)S(1)}, u32[]{:S(2)}, u32[]{:S(2)}) async-start(f32[32,320,16]{1,2,0:T(8,128)} %copy.358), calls=%async_computation.1 | async-start | bytes 1572864 | tf_op jit(solution)/shard_map/all_to_all | solution.py:72
  145.0 6.8 %fusion.117 = f32[4,5,4,4,4,128]{5,1,4,3,2,0:T(8,128)} fusion(f32[4,5,4,4,4,128]{5,1,4,3,2,0:T(8,128)} %fusion.126, f32[4,5,4,1,4,128]{5,1,4,2,0,3:T(8,128)} %slice_bitcast_fusion.1, f32[4,5,4,4,128]{1,3,4,2,0:T(4,128)} %bitcast_subtract_fusion.6, f32[1,5,5]{2,0,1:T(1,128)S(1)} %get-tuple-element.177), kind=kOutput, calls=%fused_computation.95 | convolution fusion | flops 2539595 | bytes 4718692 | tf_op jit(solution)/shard_map/wv,tvabe->twabe/dot_general | solution.py:87
  152.8 8.9 %fusion.108 = f32[4,5,4,4,4,128]{5,1,4,3,2,0:T(8,128)} fusion(f32[4,5,4,4,4,128]{5,1,4,3,2,0:T(8,128)} %fusion.117, f32[4,5,4,4,1,128]{5,1,3,2,0,4:T(8,128)S(1)} %slice_bitcast_fusion, f32[4,5,4,4,128]{1,3,2,0,4:T(4,128)} %bitcast_subtract_fusion.5, f32[1,5,5]{2,0,1:T(1,128)S(1)} %get-tuple-element.176), kind=kOutput, calls=%fused_computation.92 | convolution fusion | flops 2539620 | bytes 4620388 | tf_op jit(solution)/shard_map/wv,tvabe->twabe/dot_general | solution.py:87
  161.7 5.6 %fusion.99 = f32[4,5,4,4,4,128]{5,1,4,3,2,0:T(8,128)} fusion(f32[4,5,4,4,4,128]{5,1,4,3,2,0:T(8,128)} %fusion.108, f32[4,5,4,4,128]{1,3,4,2,0:T(4,128)S(1)} %copy-done.4, f32[1,5,5]{2,0,1:T(1,128)S(1)} %get-tuple-element.176), kind=kOutput, calls=%fused_computation.89 | convolution fusion | flops 2539595 | bytes 688228 | tf_op jit(solution)/shard_map/wv,tvabe->twabe/dot_general | solution.py:87
  183.3 3.4 copy.461
  186.7 3.2 copy.465
  201.7 3.0 collective-permute-start.2
  204.8 3.6 %copy.459 = f32[4,5,4,1,4,128]{1,4,2,0,5,3:T(4,128)} copy(f32[4,5,4,1,4,128]{5,4,3,2,1,0:T(4,128)S(1)} %copy-done.23) | data formatting | bytes 327680
  208.4 3.2 copy.458
  211.6 7.7 %gather_fusion.8 = f32[128,4,5,4,4]{2,4,3,1,0:T(4,128)} fusion(f32[4,5,4,4,128]{1,3,4,2,0:T(4,128)} %bitcast.452, s32[1024]{0:T(1024)S(1)} %pad_clamp_fusion.3), kind=kCustom, calls=%fused_computation.8.clone | custom fusion | bytes 328192 | tf_op jit(solution)/shard_map/jit(_take)/gather | solution.py:128
  219.3 3.1 copy.386
  222.4 7.8 %gather_fusion.9 = f32[128,4,5,4,4]{2,4,3,1,0:T(4,128)} fusion(f32[4,5,4,4,128]{1,3,4,2,0:T(4,128)} %copy.386, s32[1024]{0:T(1024)S(1)} %pad_clamp_fusion.2), kind=kCustom, calls=%fused_computation.9.clone | custom fusion | bytes 328192 | tf_op jit(solution)/shard_map/jit(_take)/gather | solution.py:131
  230.1 5.8 %bitcast_subtract_fusion.2 = f32[4,5,4,4,128]{1,3,4,2,0:T(4,128)} fusion(f32[128,4,5,4,4]{2,4,3,1,0:T(4,128)} %gather_fusion.9, pred[128]{0:T(512)(128)(4,1)S(1)} %get-tuple-element.189, f32[4,5,4,1,4,128]{1,4,5,2,0,3:T(4,128)} %copy.458), kind=kLoop, calls=%fused_computation.16 | loop fusion | flops 81920 | bytes 491648 | tf_op jit(solution)/shard_map/sub | solution.py:87
  235.9 3.5 %copy.460 = f32[4,5,4,4,1,128]{1,3,5,2,0,4:T(4,128)} copy(f32[4,5,4,4,1,128]{5,4,3,2,1,0:T(1,128)S(1)} %copy-done.18) | data formatting | bytes 327680
  239.5 7.8 %gather_fusion.10 = f32[128,4,5,4,4]{2,4,3,1,0:T(4,128)} fusion(f32[4,5,4,4,128]{1,3,4,2,0:T(4,128)} %bitcast.453, s32[1024]{0:T(1024)S(1)} %pad_clamp_fusion.1), kind=kCustom, calls=%fused_computation.10.clone | custom fusion | bytes 328192 | tf_op jit(solution)/shard_map/jit(_take)/gather | solution.py:134
  247.2 7.7 %gather_fusion.11 = f32[128,4,5,4,4]{2,4,3,1,0:T(4,128)} fusion(f32[4,5,4,4,128]{1,3,4,2,0:T(4,128)} %bitcast.454, s32[1024]{0:T(1024)S(1)} %pad_clamp_fusion), kind=kCustom, calls=%fused_computation.11.clone | custom fusion | bytes 328192 | tf_op jit(solution)/shard_map/jit(_take)/gather | solution.py:137
  254.9 5.8 %bitcast_subtract_fusion = f32[4,5,4,4,128]{1,3,4,2,0:T(4,128)} fusion(f32[128,4,5,4,4]{2,4,3,1,0:T(4,128)} %gather_fusion.11, pred[128]{0:T(512)(128)(4,1)S(1)} %get-tuple-element.187, f32[4,5,4,4,1,128]{1,3,5,2,0,4:T(4,128)} %copy.460), kind=kLoop, calls=%fused_computation.12 | loop fusion | flops 81920 | bytes 491648 | tf_op jit(solution)/shard_map/sub | solution.py:87
  260.7 6.2 %all-to-all-start.2 = ((f32[4,320,128]{1,0,2:T(4,128)}), f32[4,320,128]{1,0,2:T(4,128)}, u32[]{:S(2)}, u32[]{:S(2)}) async-start(f32[4,320,128]{1,0,2:T(4,128)} %copy.398), calls=%async_computation.2 | async-start | bytes 1572864 | tf_op jit(solution)/shard_map/all_to_all | solution.py:73
  266.9 2.8 convolution_add_fusion.1
  269.8 5.8 %bitcast_subtract_fusion.3 = f32[4,5,4,4,128]{1,3,2,0,4:T(4,128)} fusion(f32[4,5,4,1,4,128]{1,4,2,0,5,3:T(4,128)} %copy.459, f32[128,4,5,4,4]{2,4,3,1,0:T(4,128)} %gather_fusion.8, pred[128]{0:T(512)(128)(4,1)S(1)} %get-tuple-element.190), kind=kLoop, calls=%fused_computation.19 | loop fusion | flops 81920 | bytes 491648 | tf_op jit(solution)/shard_map/sub | solution.py:87
  277.2 3.1 bitcast_subtract_fusion.1
  280.3 2.4 fusion.16
  298.3 6.2 %all-to-all-start.3 = ((f32[32,320,16]{1,2,0:T(8,128)}), f32[32,320,16]{1,2,0:T(8,128)}, u32[]{:S(2)}, u32[]{:S(2)}) async-start(f32[32,320,16]{1,2,0:T(8,128)} %copy.401), calls=%async_computation.3 | async-start | bytes 1572864 | tf_op jit(solution)/shard_map/all_to_all | solution.py:72
  304.5 9.1 %fusion.81 = f32[4,5,4,4,4,128]{5,1,3,2,0,4:T(8,128)} fusion(f32[4,5,4,4,4,128]{5,1,3,2,0,4:T(8,128)} %fusion.138, f32[4,5,4,4,128]{1,3,2,0,4:T(4,128)} %bitcast_subtract_fusion.3, f32[1,5,5]{2,0,1:T(1,128)S(1)} %get-tuple-element.177), kind=kOutput, calls=%fused_computation.83 | convolution fusion | flops 2539620 | bytes 4718692 | tf_op jit(solution)/shard_map/wv,tvabe->twabe/dot_general | solution.py:87
  313.6 5.6 %fusion.75 = f32[4,5,4,4,4,128]{5,1,3,2,0,4:T(8,128)} fusion(f32[4,5,4,4,4,128]{5,1,3,2,0,4:T(8,128)} %fusion.81, f32[4,5,4,4,128]{1,3,4,2,0:T(4,128)S(1)} %copy-done.2, f32[1,5,5]{2,0,1:T(1,128)S(1)} %get-tuple-element.177), kind=kOutput, calls=%fused_computation.81 | convolution fusion | flops 2539595 | bytes 688228 | tf_op jit(solution)/shard_map/wv,tvabe->twabe/dot_general | solution.py:87
  319.2 8.0 %fusion.93 = f32[4,5,4,4,4,128]{5,1,3,2,0,4:T(8,128)} fusion(f32[4,5,4,4,4,128]{5,1,3,2,0,4:T(8,128)} %fusion.75, f32[4,5,4,4,128]{1,3,2,0,4:T(4,128)S(1)} %copy-done.6, f32[1,5,5]{2,0,1:T(1,128)S(1)} %get-tuple-element.176), kind=kOutput, calls=%fused_computation.87 | convolution fusion | flops 2539620 | bytes 688228 | tf_op jit(solution)/shard_map/wv,tvabe->twabe/dot_general | solution.py:87
  327.2 5.5 %fusion.87 = f32[4,5,4,4,4,128]{5,1,3,2,0,4:T(8,128)} fusion(f32[4,5,4,4,4,128]{5,1,3,2,0,4:T(8,128)} %fusion.93, f32[4,5,4,4,128]{1,3,4,2,0:T(4,128)S(1)} %copy-done.3, f32[1,5,5]{2,0,1:T(1,128)S(1)} %get-tuple-element.176), kind=kOutput, calls=%fused_computation.85 | convolution fusion | flops 2539595 | bytes 688228 | tf_op jit(solution)/shard_map/wv,tvabe->twabe/dot_general | solution.py:87
  332.7 2.5 copy.397
  339.5 4.0 %fusion.18 = f32[4,320,128]{2,1,0:T(8,128)} fusion(f32[4,320,128]{2,1,0:T(8,128)S(1)} %fusion.19, f32[4,320,320]{2,1,0:T(8,128)S(1)} %copy-done, f32[4,320,128]{2,1,0:T(8,128)S(1)} %copy-done.15, f32[4,320,128]{2,1,0:T(8,128)} %bitcast.461, f32[4,320,128]{2,1,0:T(8,128)} %copy.403), kind=kOutput, calls=%fused_computation.53 | convolution fusion | flops 629637120 | bytes 4915200 | tf_op jit(solution)/shard_map/tpq,tqe->tpe/dot_general | solution.py:160
  (166 shorter events, 91.8 us)
Async XLA Ops:
  0.6 172.7 %copy-start = (f32[4,320,320]{2,1,0:T(8,128)S(1)}, f32[4,320,320]{2,1,0:T(8,128)}, u32[]{:S(2)}) copy-start(f32[4,320,320]{2,1,0:T(8,128)} %param.38) | copy-start | bytes 4915204
  0.6 21.4 %copy-start.28 = (f32[4,4,1,1,1,1]{1,0,5,4,3,2:T(4,128)S(1)}, f32[4,4,1,1,1,1]{1,0,5,4,3,2:T(4,128)}, u32[]{:S(2)}) copy-start(f32[4,4,1,1,1,1]{1,0,5,4,3,2:T(4,128)} %constant.421) | copy-start | bytes 196
  0.7 12.6 %copy-start.1 = (f32[4,320,128]{2,1,0:T(8,128)S(1)}, f32[4,320,128]{2,1,0:T(8,128)}, u32[]{:S(2)}) copy-start(f32[4,320,128]{2,1,0:T(8,128)} %param.35) | copy-start | bytes 1966084
  6.7 20.8 %copy-start.29 = (s32[4,1,64]{2,1,0:T(1,128)S(1)}, s32[4,1,64]{2,1,0:T(1,128)}, u32[]{:S(2)}) copy-start(s32[4,1,64]{2,1,0:T(1,128)} %param.40) | copy-start | bytes 3076
  7.5 110.7 %collective-permute-start.1 = (f32[4,80,64]{2,1,0:T(8,128)}, f32[4,80,64]{2,1,0:T(8,128)}, u32[]{:S(2)}, u32[]{:S(2)}) collective-permute-start(f32[4,80,64]{2,1,0:T(8,128)} %select_bitcast_fusion.1), channel_id=1, source_target_pairs={{1,0},{2,1},{3,2},{5,4},{6,5},{7,6},{9,8},{10,9},{11,10},{13,12},{... | collective-permute-start | bytes 245768 | tf_op jit(solution)/shard_map/ppermute | solution.py:28
  9.5 18.9 %copy-start.31 = (s32[4,64]{1,0:T(4,128)S(1)}, s32[4,64]{1,0:T(4,128)}, u32[]{:S(2)}) copy-start(s32[4,64]{1,0:T(4,128)} %param.39) | copy-start | bytes 3076
  10.2 104.2 %collective-permute-start = (f32[4,80,64]{1,2,0:T(8,128)}, f32[4,80,64]{1,2,0:T(8,128)S(1)}, u32[]{:S(2)}, u32[]{:S(2)}) collective-permute-start(f32[4,80,64]{1,2,0:T(8,128)} %copy.324), channel_id=1, source_target_pairs={{0,1},{1,2},{2,3},{4,5},{5,6},{6,7},{8,9},{9,10},{10,11},{12,13},{... | collective-permute-start | bytes 245768 | tf_op jit(solution)/shard_map/ppermute | solution.py:25
  14.4 118.0 %all-to-all-start = ((f32[4,320,128]{1,0,2:T(4,128)}), f32[4,320,128]{1,0,2:T(4,128)}, u32[]{:S(2)}, u32[]{:S(2)}) async-start(f32[4,320,128]{1,0,2:T(4,128)} %copy.355), calls=%async_computation | async-start | bytes 1572864 | tf_op jit(solution)/shard_map/all_to_all | solution.py:73
  29.8 8.8 %copy-start.30 = (f32[3,5,5]{2,0,1:T(4,128)S(1)}, f32[3,5,5]{2,0,1:T(4,128)}, u32[]{:S(2)}) copy-start(f32[3,5,5]{2,0,1:T(4,128)} %param.37) | copy-start | bytes 904
  44.9 1.0 copy-start.10
  45.9 8.9 %copy-start.20 = (f32[4,5,4,4,128]{4,3,2,1,0:T(4,128)S(1)}, f32[4,5,4,4,128]{4,3,2,1,0:T(4,128)}, u32[]{:S(2)}) copy-start(f32[4,5,4,4,128]{4,3,2,1,0:T(4,128)} %get-tuple-element.161) | copy-start | bytes 491524
  50.5 7.5 %copy-start.19 = (f32[4,5,4,4,1,128]{5,4,3,2,1,0:T(1,128)S(1)}, f32[4,5,4,4,1,128]{5,4,3,2,1,0:T(1,128)}, u32[]{:S(2)}) copy-start(f32[4,5,4,4,1,128]{5,4,3,2,1,0:T(1,128)} %get-tuple-element.159) | copy-start | bytes 491524
  98.6 5.9 %copy-start.9 = (f32[4,5,4,1,4,128]{1,4,2,0,5,3:T(4,128)S(1)}, f32[4,5,4,1,4,128]{1,4,2,0,5,3:T(4,128)}, u32[]{:S(2)}) copy-start(f32[4,5,4,1,4,128]{1,4,2,0,5,3:T(4,128)} %copy.451) | copy-start | bytes 491524
  98.6 7.4 %copy-start.12 = (f32[128,4,5,4,4]{2,4,3,1,0:T(4,128)S(1)}, f32[128,4,5,4,4]{2,4,3,1,0:T(4,128)}, u32[]{:S(2)}) copy-start(f32[128,4,5,4,4]{2,4,3,1,0:T(4,128)} %gather_fusion.2) | copy-start | bytes 491524
  106.0 3.1 copy-start.7
  106.0 5.0 %copy-start.13 = (f32[128,4,5,4,4]{2,4,3,1,0:T(4,128)S(1)}, f32[128,4,5,4,4]{2,4,3,1,0:T(4,128)}, u32[]{:S(2)}) copy-start(f32[128,4,5,4,4]{2,4,3,1,0:T(4,128)} %gather_fusion.4) | copy-start | bytes 491524
  111.0 7.2 %copy-start.24 = (f32[4,5,1,4,4,64]{5,4,3,1,0,2:T(4,128)S(1)}, f32[4,5,1,4,4,64]{5,4,3,1,0,2:T(4,128)}, u32[]{:S(2)}) copy-start(f32[4,5,1,4,4,64]{5,4,3,1,0,2:T(4,128)} %get-tuple-element.172) | copy-start | bytes 245764
  111.0 7.2 %copy-start.25 = (f32[4,5,1,4,4,64]{5,4,3,1,0,2:T(4,128)S(1)}, f32[4,5,1,4,4,64]{5,4,3,1,0,2:T(4,128)}, u32[]{:S(2)}) copy-start(f32[4,5,1,4,4,64]{5,4,3,1,0,2:T(4,128)} %get-tuple-element.175) | copy-start | bytes 245764
  117.1 6.7 %copy-start.8 = (f32[4,5,4,4,128]{1,3,2,0,4:T(4,128)S(1)}, f32[4,5,4,4,128]{1,3,2,0,4:T(4,128)}, u32[]{:S(2)}) copy-start(f32[4,5,4,4,128]{1,3,2,0,4:T(4,128)} %bitcast_subtract_fusion.7) | copy-start | bytes 491524
  138.6 30.9 %all-to-all-start.1 = ((f32[32,320,16]{1,2,0:T(8,128)}), f32[32,320,16]{1,2,0:T(8,128)S(1)}, u32[]{:S(2)}, u32[]{:S(2)}) async-start(f32[32,320,16]{1,2,0:T(8,128)} %copy.358), calls=%async_computation.1 | async-start | bytes 1572864 | tf_op jit(solution)/shard_map/all_to_all | solution.py:72
  145.0 16.7 %copy-start.4 = (f32[4,5,4,4,128]{1,3,4,2,0:T(4,128)S(1)}, f32[4,5,4,4,128]{1,3,4,2,0:T(4,128)}, u32[]{:S(2)}) copy-start(f32[4,5,4,4,128]{1,3,4,2,0:T(4,128)} %bitcast_subtract_fusion.4) | copy-start | bytes 491524
  173.3 8.2 %copy-start.16 = (f32[4,320,128]{2,1,0:T(8,128)}, f32[4,320,128]{2,1,0:T(8,128)S(1)}, u32[]{:S(2)}) copy-start(f32[4,320,128]{2,1,0:T(8,128)S(1)} %add_subtract_fusion) | copy-start | bytes 1966084
  189.9 11.0 %copy-start.17 = (f32[4,5,4,4,128]{4,3,2,1,0:T(4,128)S(1)}, f32[4,5,4,4,128]{4,3,2,1,0:T(4,128)}, u32[]{:S(2)}) copy-start(f32[4,5,4,4,128]{4,3,2,1,0:T(4,128)} %get-tuple-element.158) | copy-start | bytes 491524
  193.4 11.4 %copy-start.23 = (f32[4,5,4,1,4,128]{5,4,3,2,1,0:T(4,128)S(1)}, f32[4,5,4,1,4,128]{5,4,3,2,1,0:T(4,128)}, u32[]{:S(2)}) copy-start(f32[4,5,4,1,4,128]{5,4,3,2,1,0:T(4,128)} %get-tuple-element.153) | copy-start | bytes 491524
  193.4 15.0 %copy-start.22 = (f32[4,5,4,1,4,128]{5,4,3,2,1,0:T(4,128)S(1)}, f32[4,5,4,1,4,128]{5,4,3,2,1,0:T(4,128)}, u32[]{:S(2)}) copy-start(f32[4,5,4,1,4,128]{5,4,3,2,1,0:T(4,128)} %get-tuple-element.154) | copy-start | bytes 491524
  199.6 85.1 %collective-permute-start.3 = (f32[4,80,64]{2,1,0:T(8,128)}, f32[4,80,64]{2,1,0:T(8,128)}, u32[]{:S(2)}, u32[]{:S(2)}) collective-permute-start(f32[4,80,64]{2,1,0:T(8,128)} %select_bitcast_fusion), channel_id=1, source_target_pairs={{1,0},{2,1},{3,2},{5,4},{6,5},{7,6},{9,8},{10,9},{11,10},{13,12},{... | collective-permute-start | bytes 245768 | tf_op jit(solution)/shard_map/ppermute | solution.py:28
  201.7 80.9 %collective-permute-start.2 = (f32[4,80,64]{1,2,0:T(8,128)S(1)}, f32[4,80,64]{1,2,0:T(8,128)S(1)}, u32[]{:S(2)}, u32[]{:S(2)}) collective-permute-start(f32[4,80,64]{1,2,0:T(8,128)S(1)} %copy.370), channel_id=1, source_target_pairs={{0,1},{1,2},{2,3},{4,5},{5,6},{6,7},{8,9},{9,10},{10,11},{12,13},{... | collective-permute-start | bytes 245768 | tf_op jit(solution)/shard_map/ppermute | solution.py:25
  204.8 14.5 %copy-start.21 = (f32[4,5,4,4,128]{4,3,2,1,0:T(4,128)S(1)}, f32[4,5,4,4,128]{4,3,2,1,0:T(4,128)}, u32[]{:S(2)}) copy-start(f32[4,5,4,4,128]{4,3,2,1,0:T(4,128)} %get-tuple-element.152) | copy-start | bytes 491524
  230.1 5.8 %copy-start.18 = (f32[4,5,4,4,1,128]{5,4,3,2,1,0:T(1,128)S(1)}, f32[4,5,4,4,1,128]{5,4,3,2,1,0:T(1,128)}, u32[]{:S(2)}) copy-start(f32[4,5,4,4,1,128]{5,4,3,2,1,0:T(1,128)} %get-tuple-element.150) | copy-start | bytes 491524
  260.7 29.4 %all-to-all-start.2 = ((f32[4,320,128]{1,0,2:T(4,128)}), f32[4,320,128]{1,0,2:T(4,128)}, u32[]{:S(2)}, u32[]{:S(2)}) async-start(f32[4,320,128]{1,0,2:T(4,128)} %copy.398), calls=%async_computation.2 | async-start | bytes 1572864 | tf_op jit(solution)/shard_map/all_to_all | solution.py:73
  269.7 5.9 %copy-start.5 = (f32[4,5,4,4,1,128]{1,3,2,0,5,4:T(4,128)S(1)}, f32[4,5,4,4,1,128]{1,3,2,0,5,4:T(4,128)}, u32[]{:S(2)}) copy-start(f32[4,5,4,4,1,128]{1,3,2,0,5,4:T(4,128)} %copy.461) | copy-start | bytes 491524
  269.7 7.4 %copy-start.11 = (f32[128,4,5,4,4]{2,4,3,1,0:T(4,128)S(1)}, f32[128,4,5,4,4]{2,4,3,1,0:T(4,128)}, u32[]{:S(2)}) copy-start(f32[128,4,5,4,4]{2,4,3,1,0:T(4,128)} %gather_fusion.10) | copy-start | bytes 491524
  277.2 3.1 copy-start.14
  280.3 4.5 %copy-start.26 = (f32[4,5,1,4,4,64]{5,4,3,1,0,2:T(4,128)S(1)}, f32[4,5,1,4,4,64]{5,4,3,1,0,2:T(4,128)}, u32[]{:S(2)}) copy-start(f32[4,5,1,4,4,64]{5,4,3,1,0,2:T(4,128)} %get-tuple-element.168) | copy-start | bytes 245764
  280.3 4.5 %copy-start.27 = (f32[4,5,1,4,4,64]{5,4,3,1,0,2:T(4,128)S(1)}, f32[4,5,1,4,4,64]{5,4,3,1,0,2:T(4,128)}, u32[]{:S(2)}) copy-start(f32[4,5,1,4,4,64]{5,4,3,1,0,2:T(4,128)} %get-tuple-element.171) | copy-start | bytes 245764
  298.3 36.9 %all-to-all-start.3 = ((f32[32,320,16]{1,2,0:T(8,128)}), f32[32,320,16]{1,2,0:T(8,128)}, u32[]{:S(2)}, u32[]{:S(2)}) async-start(f32[32,320,16]{1,2,0:T(8,128)} %copy.401), calls=%async_computation.3 | async-start | bytes 1572864 | tf_op jit(solution)/shard_map/all_to_all | solution.py:72
  304.5 9.1 %copy-start.2 = (f32[4,5,4,4,128]{1,3,4,2,0:T(4,128)S(1)}, f32[4,5,4,4,128]{1,3,4,2,0:T(4,128)}, u32[]{:S(2)}) copy-start(f32[4,5,4,4,128]{1,3,4,2,0:T(4,128)} %bitcast_subtract_fusion.2) | copy-start | bytes 491524
  304.5 14.7 %copy-start.6 = (f32[4,5,4,4,128]{1,3,2,0,4:T(4,128)S(1)}, f32[4,5,4,4,128]{1,3,2,0,4:T(4,128)}, u32[]{:S(2)}) copy-start(f32[4,5,4,4,128]{1,3,2,0,4:T(4,128)} %bitcast_subtract_fusion.1) | copy-start | bytes 491524
  313.6 13.6 %copy-start.3 = (f32[4,5,4,4,128]{1,3,4,2,0:T(4,128)S(1)}, f32[4,5,4,4,128]{1,3,4,2,0:T(4,128)}, u32[]{:S(2)}) copy-start(f32[4,5,4,4,128]{1,3,4,2,0:T(4,128)} %bitcast_subtract_fusion) | copy-start | bytes 491524
  327.2 12.3 %copy-start.15 = (f32[4,320,128]{2,1,0:T(8,128)S(1)}, f32[4,320,128]{2,1,0:T(8,128)}, u32[]{:S(2)}) copy-start(f32[4,320,128]{2,1,0:T(8,128)} %param.36) | copy-start | bytes 1966084
where the time goes:
time: 349 us; the launch traced here: 344 us
  local copies, waits for them, and re-layouts  163 us (47%)
  matrix products  97.3 us (28%)
  other arithmetic  47.3 us (14%)
  starting transfers between devices  35.1 us (10%)
    dot_general x12, matrix products, face_term(): jnp.einsum('wv,tvabe->twabe', matrix, plus - minus, precision=lax.Precisi...  62.8 us
    unnamed x80, local copies, waits for them, and re-layouts  43.5 us
    sub x10, other arithmetic, face_term(): plus - minus  41.3 us
    gather x2, local copies, waits for them, and re-layouts, space_residual(): jnp.take(high_z, neighbours[2], axis=4)  15.5 us
    gather x2, local copies, waits for them, and re-layouts, space_residual(): jnp.take(low_y, neighbours[1], axis=4)  15.5 us
    gather x2, local copies, waits for them, and re-layouts, space_residual(): jnp.take(low_z, neighbours[3], axis=4)  15.5 us
    gather x2, local copies, waits for them, and re-layouts, space_residual(): jnp.take(high_y, neighbours[0], axis=4)  15.4 us
    all_to_all x2, starting transfers between devices, time_rates(): lax.all_to_all(field, 'inst', split_axis=2, concat_axis=0, tiled=True)  13.9 us
  transfers between devices with their start and end apart: 8, of which 0 were waited for; matrix products, arithmetic and copies ran while one was open for 70% of the time, Pallas kernels for 0%

commit v1 on v0

v1 whole, which is shorter than its diff:
```python
import functools
import math

import jax
import jax.numpy as jnp
import numpy as np
from jax import lax
from jax.experimental import pallas as pl
from jax.experimental.pallas import tpu as pltpu
from jax.sharding import PartitionSpec as P

NODE1 = 4
SWEEPS = 2
DISSIPATION = 0.6
FREQUENCY = 0.25
LANES = 128
MESH = pl.DeviceIdType.MESH
BF = jnp.bfloat16
F32 = jnp.float32


def lobatto_derivative(count_of_nodes):
    inner_point = math.sqrt(0.2)
    points = np.array([-1.0, -inner_point, inner_point, 1.0])
    bary = np.ones(count_of_nodes)
    for a in range(count_of_nodes):
        for b in range(count_of_nodes):
            if a != b:
                bary[a] = bary[a] / (points[a] - points[b])
    table = np.zeros((count_of_nodes, count_of_nodes))
    for a in range(count_of_nodes):
        for b in range(count_of_nodes):
            if a != b:
                table[a, b] = bary[b] / bary[a] / (points[a] - points[b])
        table[a, a] = -np.sum(table[a])
    return table


def node_matrices():
    n = NODE1
    scale = n * (n - 1) / 4.0
    der = lobatto_derivative(n).astype(np.float32).astype(np.float64)
    eye = np.eye(n)
    low, high = np.zeros((n, n)), np.zeros((n, n))
    low[0, 0] = 1.0
    high[n - 1, n - 1] = 1.0
    to_low, to_high = np.zeros((n, n)), np.zeros((n, n))
    to_low[0, n - 1] = 1.0
    to_high[n - 1, 0] = 1.0

    def place(m, d):
        parts = [eye, eye, eye]
        parts[d] = m
        return np.kron(np.kron(parts[0], parts[1]), parts[2])

    own = [place(der + scale * (low - high), d) for d in range(3)]
    own.append(DISSIPATION * scale * sum(place(low + high, d) for d in range(3)))
    for d in range(3):
        own.append(place(scale * (to_high - to_low), d))
        own.append(-DISSIPATION * scale * place(to_high + to_low, d))
    return np.stack(own).astype(np.float32)


def time_weights(count):
    half = count // 2
    d = np.zeros(count)
    for m in range(1, count):
        d[m] = 0.5 * FREQUENCY * (-1.0) ** m / math.tan(math.pi * m / count)
    d[half] = 0.0
    plus = np.zeros((half, half))
    minus = np.zeros((half, half))
    for t in range(half):
        for s in range(half):
            a, b = d[(t - s) % count], d[(t - s + half) % count]
            plus[t, s] = 0.5 * (a + b)
            minus[t, s] = 0.5 * (a - b)
    return plus, minus


def split(x):
    hi = x.astype(BF)
    return hi, (x - hi.astype(F32)).astype(BF)


def mm(a, b):
    return jnp.dot(a, b, preferred_element_type=F32)


def kernel(
    cfg, flux, nodes, cross, match, state, forcing_hbm, jac_hbm, res_hbm, upd_hbm,
    xbuf, ybuf, dbuf, halo, match_up, v1, spat, forc, jac, jcat, vh, vl, wh, wl, py, pz, pb, pa,
    fsend, frecv, bsend, brecv, hsend, hrecv, msend, mrecv, lsem,
):
    n, ns, T, width, rows, chunks, crow, count, cells = cfg
    block = width * 64
    me = lax.axis_index("inst")
    sp = lax.axis_index("space")
    right, left = lax.rem(sp + 1, ns), lax.rem(sp + ns - 1, ns)
    peers = [lax.rem(me + k, n) for k in range(1, n)]

    load_f = pltpu.make_async_copy(forcing_hbm, forc, lsem.at[0])
    load_j = pltpu.make_async_copy(jac_hbm, jac, lsem.at[1])
    load_f.start()
    load_j.start()

    barrier = pltpu.get_barrier_semaphore()
    for p in peers:
        pl.semaphore_signal(barrier, inc=1, device_id={"inst": p}, device_id_type=MESH)
    for p in (right, left):
        pl.semaphore_signal(barrier, inc=1, device_id={"space": p}, device_id_type=MESH)
    pl.semaphore_wait(barrier, n + 1)

    padded = n * rows != block
    exact0 = state
    if padded:
        for t in range(T):
            v1[0, t, 0:block, :] = state[t]
            v1[0, t, block:, :] = jnp.zeros((n * rows - block, LANES), F32)
            v1[1, t, block:, :] = jnp.zeros((n * rows - block, LANES), F32)
        exact0 = v1.at[0]

    def forward(sweep, src, k, c):
        p = peers[k]
        return pltpu.make_async_remote_copy(
            src_ref=src.at[:, pl.ds(pl.multiple_of(p * rows + c * crow, 8), crow), :],
            dst_ref=xbuf.at[sweep, pl.ds(me * T, T), pl.ds(c * crow, crow), :],
            send_sem=fsend.at[sweep, k, c],
            recv_sem=frecv.at[sweep, k, c],
            device_id={"inst": p},
            device_id_type=MESH,
        )

    def backward(sweep, k, c):
        p = peers[k]
        return pltpu.make_async_remote_copy(
            src_ref=ybuf.at[sweep, pl.ds(p * T, T), pl.ds(c * crow, crow), :],
            dst_ref=dbuf.at[sweep, :, pl.ds(pl.multiple_of(me * rows + c * crow, 8), crow), :],
            send_sem=bsend.at[sweep, k, c],
            recv_sem=brecv.at[sweep, k, c],
            device_id={"inst": p},
            device_id_type=MESH,
        )

    def halos(sweep, src):
        out = []
        for t in range(T):
            for v in range(width):
                up = v * 64 + 48
                down = v * 64
                out.append(pltpu.make_async_remote_copy(
                    src_ref=src.at[t, pl.ds(up, 16), :],
                    dst_ref=halo.at[sweep, 0, t, pl.ds(v * 16, 16), :],
                    send_sem=hsend.at[sweep, 0, t * width + v],
                    recv_sem=hrecv.at[sweep, 0, t * width + v],
                    device_id={"space": right}, device_id_type=MESH))
                out.append(pltpu.make_async_remote_copy(
                    src_ref=src.at[t, pl.ds(down, 16), :],
                    dst_ref=halo.at[sweep, 1, t, pl.ds(v * 16, 16), :],
                    send_sem=hsend.at[sweep, 1, t * width + v],
                    recv_sem=hrecv.at[sweep, 1, t * width + v],
                    device_id={"space": left}, device_id_type=MESH))
        return out

    send_match = pltpu.make_async_remote_copy(
        src_ref=match, dst_ref=match_up, send_sem=msend.at[0], recv_sem=mrecv.at[0],
        device_id={"space": left}, device_id_type=MESH)

    plus, minus = time_weights(count)
    half = count // 2

    def derive(sweep, c):
        def group(g, _):
            at = pl.ds(pl.multiple_of(c * crow + g * 8, 8), 8)
            low = [xbuf[sweep, s, at, :] for s in range(half)]
            high = [xbuf[sweep, s + half, at, :] for s in range(half)]
            sums = [a + b for a, b in zip(low, high)]
            diffs = [a - b for a, b in zip(low, high)]
            for t in range(half):
                acc, dif = None, None
                for s in range(half):
                    if abs(plus[t, s]) > 1e-12:
                        term = sums[s] * float(plus[t, s])
                        acc = term if acc is None else acc + term
                    if abs(minus[t, s]) > 1e-12:
                        term = diffs[s] * float(minus[t, s])
                        dif = term if dif is None else dif + term
                ybuf[sweep, t, at, :] = acc + dif
                ybuf[sweep, t + half, at, :] = acc - dif
            return 0
        lax.fori_loop(0, crow // 8, group, 0)

    src_row = lax.broadcasted_iota(jnp.int32, (LANES, LANES), 0)
    dst_col = lax.broadcasted_iota(jnp.int32, (LANES, LANES), 1)

    def onehot(mask):
        return jnp.where(mask, 1.0, 0.0).astype(F32)

    def build_weights():
        lane_var = lax.broadcasted_iota(jnp.int32, (1, block), 1) // 64
        tiles = [jnp.concatenate([nodes[i]] * width, axis=1) for i in range(10)]
        for w in range(width):
            fe = []
            for d in range(3):
                row = jnp.zeros((1, block), F32)
                for v in range(width):
                    row = jnp.where(lane_var == v, flux[d, w, v], row)
                fe.append(row)
            same = jnp.where(lane_var == w, 1.0, 0.0)
            parts = [fe[0] * tiles[0] + fe[1] * tiles[1] + fe[2] * tiles[2] + same * tiles[3]]
            for d in range(3):
                parts.append(fe[d] * tiles[4 + 2 * d] + same * tiles[5 + 2 * d])
            hi, lo = split(jnp.concatenate(parts, axis=1))
            wh[w * 64:(w + 1) * 64, :] = hi
            wl[w * 64:(w + 1) * 64, :] = lo

    def build_moves():
        layer = (lax.broadcasted_iota(jnp.int32, (1, LANES), 1) // cells) * cells
        for f in range(4):
            nb = cross[f:f + 1, :]
            nb = jnp.concatenate([nb] * (LANES // cells), axis=1) + layer
            ref = py if f < 2 else pz
            ref[(f % 2) * LANES:(f % 2 + 1) * LANES, :] = onehot(src_row == nb).astype(BF)

    def build_match():
        last = LANES - cells
        low_ok = jnp.where(sp > 0, 1.0, 0.0)
        high_ok = jnp.where(sp < ns - 1, 1.0, 0.0)
        shift_up = onehot(dst_col == src_row + cells).astype(BF)
        shift_down = onehot(src_row == dst_col + cells).astype(BF)
        for t in range(T):
            m = jnp.concatenate([match[t]] * (LANES // cells), axis=1)
            mu = jnp.concatenate([match_up[t]] * (LANES // cells), axis=1)
            pb[t, 0:LANES, :] = shift_up
            pb[t, LANES:, :] = (onehot((dst_col < cells) & (src_row == m + last)) * low_ok).astype(BF)
            pa[t, 0:LANES, :] = shift_down
            turned = onehot((dst_col < cells) & (src_row == mu + last)) * high_ok
            pa[t, LANES:, :] = turned.T.astype(BF)

    row_id = lax.broadcasted_iota(jnp.int32, (block, 1), 0)

    def as_mask(index, value):
        return jnp.where(index == value, 1.0, 0.0).astype(F32)

    mj3, mj0 = as_mask((row_id >> 2) & 3, 3), as_mask((row_id >> 2) & 3, 0)
    mk3, mk0 = as_mask(row_id & 3, 3), as_mask(row_id & 3, 0)

    def spread_cross(src, t):
        cols = slice(t * LANES, (t + 1) * LANES)
        x = src[t, 0:block, :]
        for part, out in zip(split(x), (vh, vl)):
            out[0:block, cols] = part
            wide = part.astype(F32)
            y = jnp.concatenate([wide * mj3, wide * mj0], axis=1).astype(BF)
            z = jnp.concatenate([wide * mk3, wide * mk0], axis=1).astype(BF)
            out[2 * block:3 * block, cols] = mm(y, py[...]).astype(BF)
            out[3 * block:4 * block, cols] = mm(z, pz[...]).astype(BF)

    def spread_flow(sweep, src, t):
        cols = slice(t * LANES, (t + 1) * LANES)
        own_high = jnp.concatenate([src[t, v * 64 + 48:v * 64 + 64, :] for v in range(width)], axis=0)
        own_low = jnp.concatenate([src[t, v * 64:v * 64 + 16, :] for v in range(width)], axis=0)
        high = split(jnp.concatenate([own_high, halo[sweep, 0, t]], axis=1))
        low = split(jnp.concatenate([own_low, halo[sweep, 1, t]], axis=1))
        for i, out in enumerate((vh, vl)):
            ub = mm(high[i], pb[t]).astype(BF)
            ua = mm(low[i], pa[t]).astype(BF)
            for v in range(width):
                base = block + v * 64
                out[base:base + 16, cols] = ua[v * 16:(v + 1) * 16]
                out[base + 48:base + 64, cols] = ub[v * 16:(v + 1) * 16]

    def clear_middle():
        for out in (vh, vl):
            for v in range(width):
                base = block + v * 64 + 16
                out[base:base + 32, :] = jnp.zeros((32, T * LANES), BF)

    def split_jac():
        load_j.wait()
        for t in range(T):
            hi, lo = split(jac[t])
            jcat[t] = jnp.concatenate([hi, lo, hi], axis=1)

    def apply_space():
        total = mm(wh[...], vh[...]) + mm(wl[...], vh[...]) + mm(wh[...], vl[...])
        for t in range(T):
            spat[t] = total[:, t * LANES:(t + 1) * LANES] - forc[t]

    own_rows = pl.ds(pl.multiple_of(me * rows, 8), rows)
    own_times = pl.ds(me * T, T)

    def run_sweep(sweep, src, setup):
        jobs = list(setup)
        per = -(-len(jobs) // chunks)
        xbuf[sweep, own_times, :, :] = src[:, own_rows, :]
        for c in range(chunks):
            for job in jobs[c * per:(c + 1) * per]:
                job()
            for k in range(n - 1):
                forward(sweep, src, k, c).wait_recv()
            derive(sweep, c)
            for k in range(n - 1):
                backward(sweep, k, c).start()
        dbuf[sweep, :, own_rows, :] = ybuf[sweep, own_times, :, :]

    def finish(sweep, src, dst):
        for c in range(chunks):
            for k in range(n - 1):
                backward(sweep, k, c).wait_recv()
        for t in range(T):
            r = spat[t] + dbuf[sweep, t, 0:block, :]
            if sweep == 0:
                spat[t] = r
            hi, lo = split(r)
            step = mm(jcat[t], jnp.concatenate([hi, hi, lo], axis=0))
            dst[t, 0:block, :] = src[t, 0:block, :] - step

    for c in range(chunks):
        for k in range(n - 1):
            forward(0, exact0, k, c).start()
    first_halos = halos(0, state)
    send_match.start()
    for h in first_halos:
        h.start()

    def wait_halos(sweep, src):
        for h in halos(sweep, src):
            h.wait_recv()

    def first_halo_ready():
        send_match.wait()
        wait_halos(0, state)
        build_match()

    setup0 = [build_moves, build_weights]
    setup0 += [functools.partial(spread_cross, state, t) for t in range(T)]
    setup0 += [clear_middle, first_halo_ready]
    setup0 += [functools.partial(spread_flow, 0, state, t) for t in range(T)]
    setup0 += [split_jac]
    run_sweep(0, exact0, setup0)
    load_f.wait()
    apply_space()
    cur = v1.at[1]
    finish(0, state, cur)

    for c in range(chunks):
        for k in range(n - 1):
            forward(1, cur, k, c).start()
    for h in halos(1, cur):
        h.start()
    store_r = pltpu.make_async_copy(spat, res_hbm, lsem.at[2])
    store_r.start()
    setup1 = [functools.partial(spread_cross, cur, t) for t in range(T)]
    setup1 += [functools.partial(wait_halos, 1, cur)]
    setup1 += [functools.partial(spread_flow, 1, cur, t) for t in range(T)]
    run_sweep(1, cur, setup1)
    store_r.wait()
    apply_space()
    finish(1, cur, forc)
    store_u = pltpu.make_async_copy(forc, upd_hbm, lsem.at[3])
    store_u.start()
    for sweep, src in ((0, exact0), (1, cur)):
        for c in range(chunks):
            for k in range(n - 1):
                forward(sweep, src, k, c).wait_send()
                backward(sweep, k, c).wait_send()
        for h in halos(sweep, state if sweep == 0 else cur):
            h.wait_send()
    store_u.wait()


def body(n, ns, state, forcing, flux_jac, jacobi_inv, cross_nbr, lower_match):
    T, block, elements = state.shape
    width = flux_jac.shape[1]
    cells = cross_nbr.shape[1]
    count = n * T
    rows = -(-block // (8 * n)) * 8
    crow = 8
    chunks = rows // crow
    halo_rows = width * 16
    cfg = (n, ns, T, width, rows, chunks, crow, count, cells)
    full = n * rows
    dma = pltpu.SemaphoreType.DMA
    vmem = pl.BlockSpec(memory_space=pltpu.VMEM)
    hbm = pl.BlockSpec(memory_space=pl.ANY)
    out = jax.ShapeDtypeStruct(state.shape, F32)
    return pl.pallas_call(
        functools.partial(kernel, cfg),
        name="sweeps",
        out_shape=(out, out),
        in_specs=[pl.BlockSpec(memory_space=pltpu.SMEM), vmem, vmem, vmem, vmem, hbm, hbm],
        out_specs=(hbm, hbm),
        scratch_shapes=[
            pltpu.VMEM((SWEEPS, count, rows, LANES), F32),
            pltpu.VMEM((SWEEPS, count, rows, LANES), F32),
            pltpu.VMEM((SWEEPS, T, full, LANES), F32),
            pltpu.VMEM((SWEEPS, 2, T, halo_rows, LANES), F32),
            pltpu.VMEM((T, 1, cells), jnp.int32),
            pltpu.VMEM((2, T, full, LANES), F32),
            pltpu.VMEM((T, block, LANES), F32),
            pltpu.VMEM((T, block, LANES), F32),
            pltpu.VMEM((T, block, block), F32),
            pltpu.VMEM((T, block, 3 * block), BF),
            pltpu.VMEM((4 * block, T * LANES), BF),
            pltpu.VMEM((4 * block, T * LANES), BF),
            pltpu.VMEM((block, 4 * block), BF),
            pltpu.VMEM((block, 4 * block), BF),
            pltpu.VMEM((2 * LANES, LANES), BF),
            pltpu.VMEM((2 * LANES, LANES), BF),
            pltpu.VMEM((T, 2 * LANES, LANES), BF),
            pltpu.VMEM((T, 2 * LANES, LANES), BF),
            dma((SWEEPS, n - 1, chunks)),
            dma((SWEEPS, n - 1, chunks)),
            dma((SWEEPS, n - 1, chunks)),
            dma((SWEEPS, n - 1, chunks)),
            dma((SWEEPS, 2, T * width)),
            dma((SWEEPS, 2, T * width)),
            dma((1,)),
            dma((1,)),
            dma((4,)),
        ],
        compiler_params=pltpu.CompilerParams(
            collective_id=0, has_side_effects=True, vmem_limit_bytes=56 * 1024 * 1024
        ),
    )(flux_jac, jnp.asarray(node_matrices()), cross_nbr, lower_match, state, forcing, jacobi_inv)


def solution(mesh):
    n, ns = mesh.shape["inst"], mesh.shape["space"]
    return jax.shard_map(
        functools.partial(body, n, ns),
        mesh=mesh,
        in_specs=(
            P("inst", None, "space"),
            P("inst", None, "space"),
            P(),
            P("inst", None, None),
            P(),
            P("inst", "space", None),
        ),
        out_specs=(P("inst", None, "space"), P("inst", None, "space")),
        check_vma=False,
    )
```

time: 349 us -> 77.8 us (0.22); the launches traced: 344 us -> 77.5 us
  local copies, waits for them, and re-layouts: 163 us -> 5.24 us
  matrix products: 97.3 us -> 0 us
  Pallas kernels: 0 us -> 71.7 us
  other arithmetic: 47.3 us -> 0 us
  starting transfers between devices: 35.1 us -> 0 us
    dot_general x28 -> x0, matrix products: 97.3 us -> none  [the longest x12 62.8 us: face_term(): jnp.einsum('wv,tvabe->twabe', matrix, plus - minus, precision=lax.Precisi...]
    pallas_call x0 -> x1, Pallas kernels: none -> 71.7 us  [body(): pl.pallas_call(functools.partial(kernel, cfg), name='sweeps', out_shape=(...]
    gather x18 -> x0, local copies, waits for them, and re-layouts: 71.4 us -> none  [the longest x2 15.5 us: space_residual(): jnp.take(high_z, neighbours[2], axis=4)]
    sub x11 -> x0, other arithmetic: 42.7 us -> none  [the longest x10 41.3 us: face_term(): plus - minus]
    unnamed x80 -> x3, local copies, waits for them, and re-layouts: 43.5 us -> 5.24 us
    all_to_all x4 -> x0, starting transfers between devices: 26.4 us -> none  [the longest x2 13.9 us: time_rates(): lax.all_to_all(field, 'inst', split_axis=2, concat_axis=0, tiled=True)]
    squeeze x12 -> x0, local copies, waits for them, and re-layouts: 17.6 us -> none  [the longest x4 7.99 us: space_residual(): low_y = reshaped_array[:, :, :, 0]]
    all_to_all x10 -> x0, local copies, waits for them, and re-layouts: 14.4 us -> none  [the longest x6 7.73 us: time_rates(): lax.all_to_all(field, 'inst', split_axis=2, concat_axis=0, tiled=True)]
  transfers between devices with their start and end apart: 8 -> 0, of which waited for: 0 -> 0; matrix products, arithmetic and copies ran while one was open for 70% -> 0% of each run, Pallas kernels for 0% -> 0%
where the time goes in v1:
time: 77.8 us; the launch traced here: 77.5 us
  Pallas kernels  71.7 us (92%)
  local copies, waits for them, and re-layouts  5.24 us (7%)
    pallas_call x1, Pallas kernels, body(): pl.pallas_call(functools.partial(kernel, cfg), name='sweeps', out_shape=(...  71.7 us
    unnamed x3, local copies, waits for them, and re-layouts  5.24 us

profile of v1, /device:TPU:0, one launch (start us, length us, event | category | flops | bytes accessed | tf_op | source)
XLA Modules:
  0.0 77.5 jit_solution(16849394514014737377)
XLA Ops:
  0.6 1.3 %copy.9.flux = f32[3,5,5]{2,1,0:T(8,128)} copy(f32[3,5,5]{2,0,1:T(4,128)} %param.9) | data formatting | bytes 600 | tf_op args[2]
  1.9 71.7 %sweeps.1 = (f32[4,320,128]{2,1,0:T(8,128)}, f32[4,320,128]{2,1,0:T(8,128)}) custom-call(f32[3,5,5]{2,1,0:T(8,128)} %copy.9.flux, f32[10,64,64]{2,1,0:T(8,128)} %constant.2.clone.nodes, s32[4,64]{1,0:T(4,128)} %cross.1, s32[4,1,64]{2,1,0:T(1,128)} %match.1, f32[4,320,128]{2,1,0:T(8,128)} %state.1, f32[4,320,128]{2,1,0:T(8,128)} %forcing_hbm.1, ...), custom_call_target="tpu_custom_call" | custom-call | tf_op jit(solution)/shard_map/sweeps/pallas_call | solution.py:387
  73.6 2.0 %copy.12 = f32[4,320,128]{2,1,0:T(8,128)} copy(f32[4,320,128]{2,1,0:T(8,128)} %get-tuple-element.4) | data formatting | bytes 1310720
  75.6 2.0 %copy.13 = f32[4,320,128]{2,1,0:T(8,128)} copy(f32[4,320,128]{2,1,0:T(8,128)} %get-tuple-element.5) | data formatting | bytes 1310720

commit v2 on v1

--- a/solution.py
+++ b/solution.py
@@ -87,17 +87,23 @@
 
 
 def kernel(
-    cfg, flux, nodes, cross, match, state, forcing_hbm, jac_hbm, res_hbm, upd_hbm,
+    cfg, flux_hbm, nodes, cross, match, state_hbm, forcing_hbm, jac_hbm, res_hbm, upd_hbm,
     xbuf, ybuf, dbuf, halo, match_up, v1, spat, forc, jac, jcat, vh, vl, wh, wl, py, pz, pb, pa,
-    fsend, frecv, bsend, brecv, hsend, hrecv, msend, mrecv, lsem,
+    flux, state, fsend, frecv, bsend, brecv, hsend, hrecv, msend, mrecv, lsem,
 ):
-    n, ns, T, width, rows, chunks, crow, count, cells = cfg
+    n, ns, T, width, rows, arows, count, cells = cfg
+    brows = rows - arows
     block = width * 64
     me = lax.axis_index("inst")
     sp = lax.axis_index("space")
     right, left = lax.rem(sp + 1, ns), lax.rem(sp + ns - 1, ns)
-    peers = [lax.rem(me + k, n) for k in range(1, n)]
-
+    offsets = sorted(range(1, n), key=lambda k: (-min(k, n - k), k))
+    peers = [lax.rem(me + k, n) for k in offsets]
+
+    load_s = pltpu.make_async_copy(state_hbm, state, lsem.at[3 + T])
+    load_x = pltpu.make_async_copy(flux_hbm, flux, lsem.at[4 + T])
+    load_s.start()
+    load_x.start()
     load_f = pltpu.make_async_copy(forcing_hbm, forc, lsem.at[0])
     load_j = pltpu.make_async_copy(jac_hbm, jac, lsem.at[1])
     load_f.start()
@@ -109,6 +115,7 @@
     for p in (right, left):
         pl.semaphore_signal(barrier, inc=1, device_id={"space": p}, device_id_type=MESH)
     pl.semaphore_wait(barrier, n + 1)
+    load_s.wait()
 
     padded = n * rows != block
     exact0 = state
@@ -121,9 +128,13 @@
 
     def forward(sweep, src, k, c):
         p = peers[k]
+        if c < T:
+            t0, nt, r0, nr = c, 1, 0, arows
+        else:
+            t0, nt, r0, nr = 0, T, arows, brows
         return pltpu.make_async_remote_copy(
-            src_ref=src.at[:, pl.ds(pl.multiple_of(p * rows + c * crow, 8), crow), :],
-            dst_ref=xbuf.at[sweep, pl.ds(me * T, T), pl.ds(c * crow, crow), :],
+            src_ref=src.at[pl.ds(t0, nt), pl.ds(pl.multiple_of(p * rows + r0, 8), nr), :],
+            dst_ref=xbuf.at[sweep, pl.ds(me * T + t0, nt), pl.ds(r0, nr), :],
             send_sem=fsend.at[sweep, k, c],
             recv_sem=frecv.at[sweep, k, c],
             device_id={"inst": p},
@@ -132,14 +143,20 @@
 
     def backward(sweep, k, c):
         p = peers[k]
+        if c < T:
+            t0, nt, r0, nr = c, 1, arows, brows
+        else:
+            t0, nt, r0, nr = 0, T, 0, arows
         return pltpu.make_async_remote_copy(
-            src_ref=ybuf.at[sweep, pl.ds(p * T, T), pl.ds(c * crow, crow), :],
-            dst_ref=dbuf.at[sweep, :, pl.ds(pl.multiple_of(me * rows + c * crow, 8), crow), :],
+            src_ref=ybuf.at[sweep, pl.ds(p * T + t0, nt), pl.ds(r0, nr), :],
+            dst_ref=dbuf.at[sweep, pl.ds(t0, nt), pl.ds(pl.multiple_of(me * rows + r0, 8), nr), :],
             send_sem=bsend.at[sweep, k, c],
             recv_sem=brecv.at[sweep, k, c],
             device_id={"inst": p},
             device_id_type=MESH,
         )
+
+    everyone = range(n - 1)
 
     def halos(sweep, src):
         out = []
@@ -168,9 +185,9 @@
     plus, minus = time_weights(count)
     half = count // 2
 
-    def derive(sweep, c):
+    def derive(sweep, first, size):
         def group(g, _):
-            at = pl.ds(pl.multiple_of(c * crow + g * 8, 8), 8)
+            at = pl.ds(pl.multiple_of(first + g * 8, 8), 8)
             low = [xbuf[sweep, s, at, :] for s in range(half)]
             high = [xbuf[sweep, s + half, at, :] for s in range(half)]
             sums = [a + b for a, b in zip(low, high)]
@@ -187,7 +204,7 @@
                 ybuf[sweep, t, at, :] = acc + dif
                 ybuf[sweep, t + half, at, :] = acc - dif
             return 0
-        lax.fori_loop(0, crow // 8, group, 0)
+        lax.fori_loop(0, size // 8, group, 0)
 
     src_row = lax.broadcasted_iota(jnp.int32, (LANES, LANES), 0)
     dst_col = lax.broadcasted_iota(jnp.int32, (LANES, LANES), 1)
@@ -203,7 +220,7 @@
             for d in range(3):
                 row = jnp.zeros((1, block), F32)
                 for v in range(width):
-                    row = jnp.where(lane_var == v, flux[d, w, v], row)
+                    row = jnp.where(lane_var == v, flux[d, w:w + 1, v:v + 1], row)
                 fe.append(row)
             same = jnp.where(lane_var == w, 1.0, 0.0)
             parts = [fe[0] * tiles[0] + fe[1] * tiles[1] + fe[2] * tiles[2] + same * tiles[3]]
@@ -289,39 +306,43 @@
     own_rows = pl.ds(pl.multiple_of(me * rows, 8), rows)
     own_times = pl.ds(me * T, T)
 
-    def run_sweep(sweep, src, setup):
-        jobs = list(setup)
-        per = -(-len(jobs) // chunks)
+    def run_sweep(sweep, src, before, between):
         xbuf[sweep, own_times, :, :] = src[:, own_rows, :]
-        for c in range(chunks):
-            for job in jobs[c * per:(c + 1) * per]:
-                job()
-            for k in range(n - 1):
+        for job in before:
+            job()
+        for c in range(T):
+            for k in everyone:
                 forward(sweep, src, k, c).wait_recv()
-            derive(sweep, c)
-            for k in range(n - 1):
+        derive(sweep, 0, arows)
+        for k in everyone:
+            backward(sweep, k, T).start()
+        for job in between:
+            job()
+        for k in everyone:
+            forward(sweep, src, k, T).wait_recv()
+        derive(sweep, arows, brows)
+        for c in range(T):
+            for k in everyone:
                 backward(sweep, k, c).start()
         dbuf[sweep, :, own_rows, :] = ybuf[sweep, own_times, :, :]
 
-    def finish(sweep, src, dst):
-        for c in range(chunks):
-            for k in range(n - 1):
-                backward(sweep, k, c).wait_recv()
-        for t in range(T):
+    def finish(sweep, src, dst, after):
+        for k in everyone:
+            backward(sweep, k, T).wait_recv()
+        for t in range(T):
+            for k in everyone:
+                backward(sweep, k, t).wait_recv()
             r = spat[t] + dbuf[sweep, t, 0:block, :]
             if sweep == 0:
                 spat[t] = r
             hi, lo = split(r)
             step = mm(jcat[t], jnp.concatenate([hi, hi, lo], axis=0))
             dst[t, 0:block, :] = src[t, 0:block, :] - step
-
-    for c in range(chunks):
-        for k in range(n - 1):
-            forward(0, exact0, k, c).start()
-    first_halos = halos(0, state)
-    send_match.start()
-    for h in first_halos:
-        h.start()
+            after(t)
+
+    def send_forward(sweep, src, c):
+        for k in everyone:
+            forward(sweep, src, k, c).start()
 
     def wait_halos(sweep, src):
         for h in halos(sweep, src):
@@ -332,41 +353,42 @@
         wait_halos(0, state)
         build_match()
 
-    setup0 = [build_moves, build_weights]
-    setup0 += [functools.partial(spread_cross, state, t) for t in range(T)]
-    setup0 += [clear_middle, first_halo_ready]
-    setup0 += [functools.partial(spread_flow, 0, state, t) for t in range(T)]
-    setup0 += [split_jac]
-    run_sweep(0, exact0, setup0)
-    load_f.wait()
-    apply_space()
+    for c in range(T + 1):
+        send_forward(0, exact0, c)
+    send_match.start()
+    for h in halos(0, state):
+        h.start()
+    before = [build_moves, load_x.wait, build_weights]
+    before += [functools.partial(spread_cross, state, t) for t in range(T)]
+    before += [clear_middle]
+    between = [first_halo_ready]
+    between += [functools.partial(spread_flow, 0, state, t) for t in range(T)]
+    between += [load_f.wait, apply_space, split_jac]
+    run_sweep(0, exact0, before, between)
     cur = v1.at[1]
-    finish(0, state, cur)
-
-    for c in range(chunks):
-        for k in range(n - 1):
-            forward(1, cur, k, c).start()
+    finish(0, state, cur, lambda t: send_forward(1, cur, t))
+
+    send_forward(1, cur, T)
     for h in halos(1, cur):
         h.start()
     store_r = pltpu.make_async_copy(spat, res_hbm, lsem.at[2])
     store_r.start()
-    setup1 = [functools.partial(spread_cross, cur, t) for t in range(T)]
-    setup1 += [functools.partial(wait_halos, 1, cur)]
-    setup1 += [functools.partial(spread_flow, 1, cur, t) for t in range(T)]
-    run_sweep(1, cur, setup1)
-    store_r.wait()
-    apply_space()
-    finish(1, cur, forc)
-    store_u = pltpu.make_async_copy(forc, upd_hbm, lsem.at[3])
-    store_u.start()
+    before = [functools.partial(spread_cross, cur, t) for t in range(T)]
+    between = [functools.partial(wait_halos, 1, cur)]
+    between += [functools.partial(spread_flow, 1, cur, t) for t in range(T)]
+    between += [store_r.wait, apply_space]
+    run_sweep(1, cur, before, between)
+    stores = [pltpu.make_async_copy(forc.at[t], upd_hbm.at[t], lsem.at[3 + t]) for t in range(T)]
+    finish(1, cur, forc, lambda t: stores[t].start())
     for sweep, src in ((0, exact0), (1, cur)):
-        for c in range(chunks):
-            for k in range(n - 1):
+        for c in range(T + 1):
+            for k in everyone:
                 forward(sweep, src, k, c).wait_send()
                 backward(sweep, k, c).wait_send()
         for h in halos(sweep, state if sweep == 0 else cur):
             h.wait_send()
-    store_u.wait()
+    for store in stores:
+        store.wait()
 
 
 def body(n, ns, state, forcing, flux_jac, jacobi_inv, cross_nbr, lower_match):
@@ -375,10 +397,10 @@
     cells = cross_nbr.shape[1]
     count = n * T
     rows = -(-block // (8 * n)) * 8
-    crow = 8
-    chunks = rows // crow
+    arows = -(-rows // 16) * 8
+    pieces = T + 1
     halo_rows = width * 16
-    cfg = (n, ns, T, width, rows, chunks, crow, count, cells)
+    cfg = (n, ns, T, width, rows, arows, count, cells)
     full = n * rows
     dma = pltpu.SemaphoreType.DMA
     vmem = pl.BlockSpec(memory_space=pltpu.VMEM)
@@ -388,7 +410,7 @@
         functools.partial(kernel, cfg),
         name="sweeps",
         out_shape=(out, out),
-        in_specs=[pl.BlockSpec(memory_space=pltpu.SMEM), vmem, vmem, vmem, vmem, hbm, hbm],
+        in_specs=[hbm, vmem, vmem, vmem, hbm, hbm, hbm],
         out_specs=(hbm, hbm),
         scratch_shapes=[
             pltpu.VMEM((SWEEPS, count, rows, LANES), F32),
@@ -409,15 +431,17 @@
             pltpu.VMEM((2 * LANES, LANES), BF),
             pltpu.VMEM((T, 2 * LANES, LANES), BF),
             pltpu.VMEM((T, 2 * LANES, LANES), BF),
-            dma((SWEEPS, n - 1, chunks)),
-            dma((SWEEPS, n - 1, chunks)),
-            dma((SWEEPS, n - 1, chunks)),
-            dma((SWEEPS, n - 1, chunks)),
+            pltpu.VMEM(flux_jac.shape, F32),
+            pltpu.VMEM((T, block, LANES), F32),
+            dma((SWEEPS, n - 1, pieces)),
+            dma((SWEEPS, n - 1, pieces)),
+            dma((SWEEPS, n - 1, pieces)),
+            dma((SWEEPS, n - 1, pieces)),
             dma((SWEEPS, 2, T * width)),
             dma((SWEEPS, 2, T * width)),
             dma((1,)),
             dma((1,)),
-            dma((4,)),
+            dma((5 + T,)),
         ],
         compiler_params=pltpu.CompilerParams(
             collective_id=0, has_side_effects=True, vmem_limit_bytes=56 * 1024 * 1024

time: 77.8 us -> 76 us (0.977)
  Pallas kernels: 71.7 us -> 69.9 us
    pallas_call x1, Pallas kernels: 71.7 us -> 69.9 us  [body(): pl.pallas_call(functools.partial(kernel, cfg), name='sweeps', out_shape=(...]
where the time goes in v2:
time: 76 us; the launch traced here: 75.7 us
  Pallas kernels  69.9 us (92%)
  local copies, waits for them, and re-layouts  5.24 us (7%)
    pallas_call x1, Pallas kernels, body(): pl.pallas_call(functools.partial(kernel, cfg), name='sweeps', out_shape=(...  69.9 us
    unnamed x3, local copies, waits for them, and re-layouts  5.24 us

profile of v2, /device:TPU:0, one launch (start us, length us, event | category | flops | bytes accessed | tf_op | source)
XLA Modules:
  0.0 75.7 jit_solution(6829612773311066083)
XLA Ops:
  0.6 1.3 %copy.9.flux_hbm = f32[3,5,5]{2,1,0:T(8,128)} copy(f32[3,5,5]{2,0,1:T(4,128)} %param.9) | data formatting | bytes 600 | tf_op args[2]
  1.9 69.9 %sweeps.1 = (f32[4,320,128]{2,1,0:T(8,128)}, f32[4,320,128]{2,1,0:T(8,128)}) custom-call(f32[3,5,5]{2,1,0:T(8,128)} %copy.9.flux_hbm, f32[10,64,64]{2,1,0:T(8,128)} %constant.2.clone.nodes, s32[4,64]{1,0:T(4,128)} %cross.1, s32[4,1,64]{2,1,0:T(1,128)} %match.1, f32[4,320,128]{2,1,0:T(8,128)} %state_hbm.1, f32[4,320,128]{2,1,0:T(8,128)} %forcing_hbm.1, ...), custom_call_target="tpu_custom_call" | custom-call | tf_op jit(solution)/shard_map/sweeps/pallas_call | solution.py:409
  71.8 2.0 %copy.12 = f32[4,320,128]{2,1,0:T(8,128)} copy(f32[4,320,128]{2,1,0:T(8,128)} %get-tuple-element.4) | data formatting | bytes 1310720
  73.8 2.0 %copy.13 = f32[4,320,128]{2,1,0:T(8,128)} copy(f32[4,320,128]{2,1,0:T(8,128)} %get-tuple-element.5) | data formatting | bytes 1310720
